TPU v7x, 256 devices: a whole 4x4x8 slice. The times are simulated.
256 devices in a mesh: claim: 64 (over y_hi, x, z), feat: 4 (over y_lo, core).
Axes of the slice: x: 4, y: 4 (y_hi: 2, y_lo: 2; y = y_hi * 2 + y_lo), z: 8, core: 2. Of those that a mesh axis runs over, the one named last changes fastest.
Arguments:
- block_tiles: bfloat16 [64, 4, 128, 128, 128], P('claim', 'feat'), may hold values from 0.049804688 to 1
- block_scale: float32 [64, 4, 128], P('claim', 'feat'), may hold values from 1 to 12, as said below
- row_index: int32 [64, 4, 128], P('claim', 'feat'), may hold values from 0 to 63
- col_index: int32 [64, 4, 128], P('claim', 'feat'), may hold values from 0 to 31
- start_basis: float32 [16384, 64], P('feat'), may hold values from -6 to 6
Outputs:
- claim_basis: float32 [524288, 64], P(('claim', 'feat'))
- feature_basis: float32 [16384, 64], P(('feat', 'claim'))
- bidiagonal: float32 [4, 64, 64], replicated
Inputs may be any that keep to these rules, and one draw needn't show every extreme that they name: `row_index`: row block within the device's 64 row blocks of claims; a few row blocks hold most stored blocks. `col_index`: column block within the device's 32 column blocks. `block_scale`: positive block scales.
All inputs are finite; a program needn't handle non-finite values.
Results may differ from a plain program's by a relative error of at most 0.012.
Values may be sent and summed in bfloat16 or wider, within the bound.
A program may use at most 64 MiB of HBM per device.

v0:
```python
import jax
import jax.numpy as jnp
from jax import lax
from jax.sharding import Mesh
from jax.sharding import PartitionSpec as P

BLK_ROWS = 64
HIGH = lax.Precision.HIGHEST
FINE = ("yh", "x", "z", "yl", "c")
CLAIM = ("yh", "x", "z")
FEAT = ("yl", "c")


def forward_local(block_tiles, block_scale, row_index, col_index, operand):
    edge = block_tiles.shape[-1]
    width = operand.shape[-1]
    picked = operand.reshape(-1, edge, width)[col_index]
    products = jnp.einsum("bij,bjk->bik", block_tiles, picked, preferred_element_type=jnp.float32)
    products = products * block_scale[:, None, None]
    selector = (row_index[None, :] == jnp.arange(BLK_ROWS, dtype=jnp.int32)[:, None]).astype(
        jnp.float32
    )
    summed = jnp.einsum("rb,bik->rik", selector, products, precision=HIGH)
    return summed.reshape(BLK_ROWS * edge, width)


def backward_local(block_tiles, block_scale, row_index, col_index, operand, col_count):
    edge = block_tiles.shape[-1]
    width = operand.shape[-1]
    picked = operand.reshape(-1, edge, width)[row_index]
    products = jnp.einsum("bij,bik->bjk", block_tiles, picked, preferred_element_type=jnp.float32)
    products = products * block_scale[:, None, None]
    selector = (col_index[None, :] == jnp.arange(col_count, dtype=jnp.int32)[:, None]).astype(
        jnp.float32
    )
    summed = jnp.einsum("cb,bjk->cjk", selector, products, precision=HIGH)
    return summed.reshape(col_count * edge, width)


def degree_local(block_tiles, block_scale, row_index, col_index, col_count):
    row_sums = jnp.sum(block_tiles, axis=2, dtype=jnp.float32) * block_scale[:, None]
    col_sums = jnp.sum(block_tiles, axis=1, dtype=jnp.float32) * block_scale[:, None]
    row_select = (row_index[None, :] == jnp.arange(BLK_ROWS, dtype=jnp.int32)[:, None]).astype(
        jnp.float32
    )
    col_select = (col_index[None, :] == jnp.arange(col_count, dtype=jnp.int32)[:, None]).astype(
        jnp.float32
    )
    row_part = jnp.einsum("rb,bi->ri", row_select, row_sums, precision=HIGH).reshape(-1)
    col_part = jnp.einsum("cb,bi->ci", col_select, col_sums, precision=HIGH).reshape(-1)
    return (row_part, col_part)


def gram_of(block):
    return jnp.dot(block.T, block, precision=HIGH)


def orthonormal(block, gram_total):
    factor = jnp.linalg.cholesky(gram_total)
    basis = lax.linalg.triangular_solve(
        factor, block, left_side=False, lower=True, transpose_a=True
    )
    return (basis, factor.T)


def claim_sum(value):
    part = lax.psum_scatter(value, "z", scatter_dimension=0, tiled=True)
    part = lax.psum(part, ("yh", "x"))
    return lax.all_gather(part, "z", axis=0, tiled=True)


def all_sum(value):
    value = lax.psum(value, FEAT)
    value = lax.psum(value, "z")
    return lax.psum(value, ("yh", "x"))


def claim_scatter(value):
    size_z = lax.axis_size("z")
    size_o = lax.axis_size("yh") * lax.axis_size("x")
    rows = value.shape[0] // (size_z * size_o)
    blocks = value.reshape(size_o, size_z, rows, -1).transpose(1, 0, 2, 3).reshape(value.shape)
    part = lax.psum_scatter(blocks, "z", scatter_dimension=0, tiled=True)
    return lax.psum_scatter(part, ("yh", "x"), scatter_dimension=0, tiled=True)


def per_device(block_tiles, block_scale, row_index, col_index, start_basis):
    tiles_here = block_tiles.reshape(block_tiles.shape[-3:])
    scale_here = block_scale.reshape(-1)
    rows_here = row_index.reshape(-1)
    cols_here = col_index.reshape(-1)
    edge = tiles_here.shape[-1]
    col_count = start_basis.shape[0] // edge
    claim_count = lax.axis_size(CLAIM)
    own_cols = start_basis.shape[0] // claim_count
    own_first = lax.axis_index(CLAIM) * own_cols
    row_part, col_part = degree_local(tiles_here, scale_here, rows_here, cols_here, col_count)
    col_total = claim_sum(col_part)
    col_scale = lax.rsqrt(col_total + 1.0)
    row_total = lax.psum_scatter(row_part, FEAT, scatter_dimension=0, tiled=True)
    start_total = lax.psum(gram_of(start_basis), FEAT)
    first_basis, _ = orthonormal(start_basis, start_total)
    first_operand = (col_scale[:, None] * first_basis).astype(jnp.bfloat16)
    first_partial = forward_local(tiles_here, scale_here, rows_here, cols_here, first_operand)
    first_sums = lax.psum_scatter(first_partial, FEAT, scatter_dimension=0, tiled=True)
    row_scale = lax.rsqrt(row_total + 1.0)

    def row_orthonormal(block):
        return orthonormal(block, all_sum(gram_of(block)))

    def backward_partial(basis):
        operand = (row_scale[:, None] * basis).astype(jnp.bfloat16)
        gathered = lax.all_gather(operand, FEAT, axis=0, tiled=True)
        return backward_local(tiles_here, scale_here, rows_here, cols_here, gathered, col_count)

    u_first, b_first = row_orthonormal(row_scale[:, None] * first_sums)
    summed = claim_sum(backward_partial(u_first))
    update = col_scale[:, None] * summed - jnp.dot(first_basis, b_first.T, precision=HIGH)
    v_second, a_second = orthonormal(update, lax.psum(gram_of(update), FEAT))
    scaled = (col_scale[:, None] * v_second).astype(jnp.bfloat16)
    second_partial = forward_local(tiles_here, scale_here, rows_here, cols_here, scaled)
    second_sums = lax.psum_scatter(second_partial, FEAT, scatter_dimension=0, tiled=True)
    p_second = row_scale[:, None] * second_sums - jnp.dot(u_first, a_second.T, precision=HIGH)
    u_second, b_second = row_orthonormal(p_second)
    own_sums = claim_scatter(backward_partial(u_second))
    own_scale = lax.dynamic_slice_in_dim(col_scale, own_first, own_cols, 0)
    own_second = lax.dynamic_slice_in_dim(v_second, own_first, own_cols, 0)
    q_second = own_scale[:, None] * own_sums - jnp.dot(own_second, b_second.T, precision=HIGH)
    v_output, a_third = orthonormal(q_second, all_sum(gram_of(q_second)))
    bidiagonal = jnp.stack([b_first, a_second, b_second, a_third])
    return (u_second, v_output, bidiagonal)


def solution(mesh):
    claim_n, feat_n = mesh.devices.shape
    fine = Mesh(mesh.devices.reshape(2, claim_n // 16, 8, 2, feat_n // 2), FINE)
    placed = (
        P(CLAIM, FEAT, None, None, None),
        P(CLAIM, FEAT, None),
        P(CLAIM, FEAT, None),
        P(CLAIM, FEAT, None),
        P(FEAT, None),
    )
    return jax.shard_map(
        per_device,
        mesh=fine,
        in_specs=placed,
        out_specs=(P(CLAIM + FEAT, None), P(FEAT + CLAIM, None), P()),
        check_vma=False,
    )
```

profile of v0, /device:TPU:16, one launch (start us, length us, event | category | flops | bytes accessed | tf_op | source)
XLA Modules:
  0.0 885.8 jit_solution(7263501189897861546)
XLA Ops:
  13.1 32.8 %all-reduce.1 = f32[4096]{0:T(1024)S(1)} all-reduce(f32[4096]{0:T(1024)S(1)} %convolution_bitcast_fusion.5), channel_id=3, replica_groups=mesh['yh'=2,'x'=4,'z'=8,'yl'=2,'c'=2] {'z'}, use_global_device_ids=true, to_apply=%region_3.0.clone | all-reduce | flops 4096 | bytes 32768
  47.2 21.5 %psum.91 = f32[512]{0:T(512)S(1)} all-reduce(f32[512]{0:T(512)S(1)} %dynamic-slice.3), channel_id=1, replica_groups=mesh['yh'=2,'x'=4,'z'=8,'yl'=2,'c'=2] {'yh','x'}, use_global_device_ids=true, to_apply=%region_4.0 | all-reduce | flops 512 | bytes 4096 | tf_op jit(solution)/shard_map/psum | solution.py:68
  68.6 20.8 %all-gather = f32[8,1,512]{2,1,0:T(1,128)S(1)} all-gather(f32[1,1,512]{2,1,0:T(1,128)S(1)} %bitcast.205), channel_id=1, replica_groups=mesh['yh'=2,'x'=4,'z'=8,'yl'=2,'c'=2] {'z'}, dimensions={0}, use_global_device_ids=true | all-gather | bytes 18432 | tf_op jit(solution)/shard_map/all_gather | solution.py:69
  89.7 10.9 %all-reduce.2 = (f32[64,64]{0,1:T(8,128)S(1)}, f32[8192]{0:T(1024)S(1)}) all-reduce(f32[64,64]{0,1:T(8,128)S(1)} %fusion.101, f32[8192]{0:T(1024)S(1)} %convolution_bitcast_fusion.4), channel_id=1, replica_groups=mesh['yh'=2,'x'=4,'z'=8,'yl'=2,'c'=2] {'yl','c'}, use_global_device_ids=true, to_apply=%region_5.0 | all-reduce | flops 12288 | bytes 98304 | tf_op jit(solution)/shard_map/psum | solution.py:101
  130.0 26.5 %reduce-scatter.6.cloned.1.call-done = f32[2048,64]{0,1:T(8,128)} async-done(((f32[8192,64]{0,1:T(8,128)}), f32[2048,64]{0,1:T(8,128)}) %reduce-scatter.6.cloned.1.call-update) | async-done | bytes 524304 | tf_op jit(solution)/shard_map/reduce_scatter | solution.py:105
  158.4 10.7 %psum.93 = f32[64,64]{0,1:T(8,128)S(1)} all-reduce(f32[64,64]{0,1:T(8,128)S(1)} %fusion.27), channel_id=1, replica_groups=mesh['yh'=2,'x'=4,'z'=8,'yl'=2,'c'=2] {'yl','c'}, use_global_device_ids=true, to_apply=%region_9.12 | all-reduce | flops 4096 | bytes 32768 | tf_op jit(solution)/shard_map/psum | solution.py:73
  169.1 30.2 %psum.94 = f32[64,64]{0,1:T(8,128)S(1)} all-reduce(f32[64,64]{0,1:T(8,128)S(1)} %psum.93), channel_id=1, replica_groups=mesh['yh'=2,'x'=4,'z'=8,'yl'=2,'c'=2] {'z'}, use_global_device_ids=true, to_apply=%region_10.13 | all-reduce | flops 4096 | bytes 32768 | tf_op jit(solution)/shard_map/psum | solution.py:74
  199.3 39.5 %psum.95 = f32[64,64]{0,1:T(8,128)S(1)} all-reduce(f32[64,64]{0,1:T(8,128)S(1)} %psum.94), channel_id=1, replica_groups=mesh['yh'=2,'x'=4,'z'=8,'yl'=2,'c'=2] {'yh','x'}, use_global_device_ids=true, to_apply=%region_11.14 | all-reduce | flops 4096 | bytes 32768 | tf_op jit(solution)/shard_map/psum | solution.py:75
  238.9 5.8 cholesky.100
  253.6 19.9 %all-gather.5.cloned.1.call-done = bf16[8192,64]{0,1:T(8,128)(2,1)} async-done(((bf16[2048,64]{0,1:T(8,128)(2,1)}), bf16[8192,64]{0,1:T(8,128)(2,1)}) %all-gather.5.cloned.1.call-update) | async-done | bytes 1048592 | tf_op jit(solution)/shard_map/all_gather | solution.py:113
  286.9 40.0 %reduce-scatter.8.cloned.1.call-done = f32[512,64]{0,1:T(8,128)} async-done(((f32[4096,64]{0,1:T(8,128)}), f32[512,64]{0,1:T(8,128)}) %reduce-scatter.8.cloned.1.call-update) | async-done | bytes 131088 | tf_op jit(solution)/shard_map/reduce_scatter | solution.py:67
  327.0 87.9 %all-reduce.5.cloned.1.call-done = f32[512,64]{0,1:T(8,128)} async-done(((f32[512,64]{0,1:T(8,128)}), f32[512,64]{0,1:T(8,128)}) %all-reduce.5.cloned.1.call-update) | async-done | bytes 131088 | tf_op jit(solution)/shard_map/psum | solution.py:68
  414.9 40.9 %all-gather.7.cloned.1.call-done = f32[4096,64]{0,1:T(8,128)} async-done(((f32[512,64]{0,1:T(8,128)}), f32[4096,64]{0,1:T(8,128)}) %all-gather.7.cloned.1.call-update) | async-done | bytes 1048592 | tf_op jit(solution)/shard_map/all_gather | solution.py:69
  459.7 10.7 %psum.97 = f32[64,64]{0,1:T(8,128)S(1)} all-reduce(f32[64,64]{0,1:T(8,128)S(1)} %fusion.102), channel_id=1, replica_groups=mesh['yh'=2,'x'=4,'z'=8,'yl'=2,'c'=2] {'yl','c'}, use_global_device_ids=true, to_apply=%region_14.18 | all-reduce | flops 4096 | bytes 32768 | tf_op jit(solution)/shard_map/psum | solution.py:119
  499.5 28.9 %reduce-scatter.10.cloned.1.call-done = f32[2048,64]{0,1:T(8,128)} async-done(((f32[8192,64]{0,1:T(8,128)}), f32[2048,64]{0,1:T(8,128)}) %reduce-scatter.10.cloned.1.call-update) | async-done | bytes 524304 | tf_op jit(solution)/shard_map/reduce_scatter | solution.py:122
  531.3 10.7 %psum.98 = f32[64,64]{0,1:T(8,128)S(1)} all-reduce(f32[64,64]{0,1:T(8,128)S(1)} %fusion.103), channel_id=1, replica_groups=mesh['yh'=2,'x'=4,'z'=8,'yl'=2,'c'=2] {'yl','c'}, use_global_device_ids=true, to_apply=%region_16.20 | all-reduce | flops 4096 | bytes 32768 | tf_op jit(solution)/shard_map/psum | solution.py:73
  542.0 30.2 %psum.99 = f32[64,64]{0,1:T(8,128)S(1)} all-reduce(f32[64,64]{0,1:T(8,128)S(1)} %psum.98), channel_id=1, replica_groups=mesh['yh'=2,'x'=4,'z'=8,'yl'=2,'c'=2] {'z'}, use_global_device_ids=true, to_apply=%region_17.21 | all-reduce | flops 4096 | bytes 32768 | tf_op jit(solution)/shard_map/psum | solution.py:74
  572.2 39.5 %psum.100 = f32[64,64]{0,1:T(8,128)S(1)} all-reduce(f32[64,64]{0,1:T(8,128)S(1)} %psum.99), channel_id=1, replica_groups=mesh['yh'=2,'x'=4,'z'=8,'yl'=2,'c'=2] {'yh','x'}, use_global_device_ids=true, to_apply=%region_18.22 | all-reduce | flops 4096 | bytes 32768 | tf_op jit(solution)/shard_map/psum | solution.py:75
  625.5 19.9 %all-gather.9.cloned.1.call-done = bf16[8192,64]{0,1:T(8,128)(2,1)} async-done(((bf16[2048,64]{0,1:T(8,128)(2,1)}), bf16[8192,64]{0,1:T(8,128)(2,1)}) %all-gather.9.cloned.1.call-update) | async-done | bytes 1048592 | tf_op jit(solution)/shard_map/all_gather | solution.py:113
  662.0 43.3 %reduce-scatter.12.cloned.1.call-done = f32[512,64]{1,0:T(8,128)} async-done(((f32[4096,64]{1,0:T(8,128)}), f32[512,64]{1,0:T(8,128)}) %reduce-scatter.12.cloned.1.call-update) | async-done | bytes 131088 | tf_op jit(solution)/shard_map/reduce_scatter | solution.py:83
  705.4 77.8 %reduce-scatter.14.cloned.1.call-done = f32[64,64]{1,0:T(8,128)} async-done(((f32[512,64]{1,0:T(8,128)}), f32[64,64]{1,0:T(8,128)}) %reduce-scatter.14.cloned.1.call-update) | async-done | bytes 16400 | tf_op jit(solution)/shard_map/reduce_scatter | solution.py:84
  785.2 10.3 %psum.101 = f32[64,64]{0,1:T(8,128)S(1)} all-reduce(f32[64,64]{0,1:T(8,128)S(1)} %fusion.104), channel_id=1, replica_groups=mesh['yh'=2,'x'=4,'z'=8,'yl'=2,'c'=2] {'yl','c'}, use_global_device_ids=true, to_apply=%region_21.25 | all-reduce | flops 4096 | bytes 32768 | tf_op jit(solution)/shard_map/psum | solution.py:73
  795.5 30.2 %psum.102 = f32[64,64]{0,1:T(8,128)S(1)} all-reduce(f32[64,64]{0,1:T(8,128)S(1)} %psum.101), channel_id=1, replica_groups=mesh['yh'=2,'x'=4,'z'=8,'yl'=2,'c'=2] {'z'}, use_global_device_ids=true, to_apply=%region_22.26 | all-reduce | flops 4096 | bytes 32768 | tf_op jit(solution)/shard_map/psum | solution.py:74
  825.7 39.7 %psum.103 = f32[64,64]{0,1:T(8,128)S(1)} all-reduce(f32[64,64]{0,1:T(8,128)S(1)} %psum.102), channel_id=1, replica_groups=mesh['yh'=2,'x'=4,'z'=8,'yl'=2,'c'=2] {'yh','x'}, use_global_device_ids=true, to_apply=%region_23.27 | all-reduce | flops 4096 | bytes 32768 | tf_op jit(solution)/shard_map/psum | solution.py:75
  (117 shorter events, 141.5 us)
Async XLA Ops:
  7.2 1.3 copy-start
  7.2 38.7 %copy-start.7 = (u32[256]{0:T(256)S(1)}, u32[256]{0:T(256)}, u32[]{:S(2)}) copy-start(u32[256]{0:T(256)} %constant.80) | copy-start | bytes 3076
  7.2 5.7 copy-start.5
  7.2 5.7 copy-start.3
  7.2 82.3 %copy-start.4 = (s32[1,1,128]{2,1,0:T(1,128)S(1)}, s32[1,1,128]{2,1,0:T(1,128)}, u32[]{:S(2)}) copy-start(s32[1,1,128]{2,1,0:T(1,128)} %param.12) | copy-start | bytes 1540
  7.2 149.3 %reduce-scatter.6.cloned.1.call-start = ((), (), s32[]{:S(2)}) async-start(), calls=%async_computation.5 | async-start | bytes 2621440 | tf_op jit(solution)/shard_map/reduce_scatter | solution.py:105
  126.1 2.6 copy-start.6
  128.7 144.8 %all-gather.5.cloned.1.call-start = ((), (), s32[]{:S(2)}) async-start(), calls=%async_computation.6 | async-start | bytes 1310720 | tf_op jit(solution)/shard_map/all_gather | solution.py:113
  253.6 73.4 %reduce-scatter.8.cloned.1.call-start = ((), (), s32[]{:S(2)}) async-start(), calls=%async_computation.7 | async-start | bytes 1179648 | tf_op jit(solution)/shard_map/reduce_scatter | solution.py:67
  286.8 128.0 %all-reduce.5.cloned.1.call-start = ((), (), s32[]{:S(2)}) async-start(), calls=%async_computation.8 | async-start | bytes 262144 | tf_op jit(solution)/shard_map/psum | solution.py:68
  326.9 128.9 %all-gather.7.cloned.1.call-start = ((), (), s32[]{:S(2)}) async-start(), calls=%async_computation.9 | async-start | bytes 1179648 | tf_op jit(solution)/shard_map/all_gather | solution.py:69
  414.9 113.6 %reduce-scatter.10.cloned.1.call-start = ((), (), s32[]{:S(2)}) async-start(), calls=%async_computation.10 | async-start | bytes 2621440 | tf_op jit(solution)/shard_map/reduce_scatter | solution.py:122
  483.7 1.0 copy-start.1
  496.9 31.5 %copy-start.2 = (f32[2048,64]{0,1:T(8,128)S(1)}, f32[2048,64]{0,1:T(8,128)}, u32[]{:S(2)}) copy-start(f32[2048,64]{0,1:T(8,128)} %get-tuple-element.28) | copy-start | bytes 1572868
  499.5 145.9 %all-gather.9.cloned.1.call-start = ((), (), s32[]{:S(2)}) async-start(), calls=%async_computation.11 | async-start | bytes 1310720 | tf_op jit(solution)/shard_map/all_gather | solution.py:113
  625.5 79.8 %reduce-scatter.12.cloned.1.call-start = ((), (), s32[]{:S(2)}) async-start(), calls=%async_computation.12 | async-start | bytes 2359296 | tf_op jit(solution)/shard_map/reduce_scatter | solution.py:83
  662.0 121.3 %reduce-scatter.14.cloned.1.call-start = ((), (), s32[]{:S(2)}) async-start(), calls=%async_computation.13 | async-start | bytes 294912 | tf_op jit(solution)/shard_map/reduce_scatter | solution.py:84
Sparse Core Ops, SparseCore 0:
  128.8 27.6 reduce-scatter.5
  253.7 19.8 all-gather.4
  286.9 39.9 reduce-scatter.7
  329.6 85.2 all-reduce.4
  416.5 39.2 all-gather.6
  499.6 28.7 reduce-scatter.9
  625.6 19.8 all-gather.8
  662.1 43.1 reduce-scatter.11
  709.6 73.5 reduce-scatter.13
where the time goes:
time: 890 us; the launch traced here: 886 us
  waiting for transfers between devices  385 us (43%)
  blocking collectives  338 us (38%)
  other arithmetic  64.9 us (7%)
  matrix products  55.8 us (6%)
  local copies, waits for them, and re-layouts  26.1 us (3%)
  between operations  15.8 us (2%)
    psum x3, blocking collectives, all_sum(): return lax.psum(value, ('yh', 'x'))  119 us
    psum x3, blocking collectives, all_sum(): value = lax.psum(value, 'z')  90.6 us
    psum x1, waiting for transfers between devices, claim_sum(): part = lax.psum(part, ('yh', 'x'))  87.9 us
    reduce_scatter x1, waiting for transfers between devices, claim_scatter(): return lax.psum_scatter(part, ('yh', 'x'), scatter_dimension=0, tiled=True)  77.8 us
    reduce_scatter x1, waiting for transfers between devices, claim_scatter(): part = lax.psum_scatter(blocks, 'z', scatter_dimension=0, tiled=True)  43.3 us
    all_gather x1, waiting for transfers between devices, claim_sum(): return lax.all_gather(part, 'z', axis=0, tiled=True)  40.9 us
    reduce_scatter x1, waiting for transfers between devices, claim_sum(): part = lax.psum_scatter(value, 'z', scatter_dimension=0, tiled=True)  40 us
    all_gather x2, waiting for transfers between devices, backward_partial(): gathered = lax.all_gather(operand, FEAT, axis=0, tiled=True)  39.8 us
  transfers between devices with their start and end apart: 9, of which 9 were waited for; matrix products, arithmetic and copies ran while one was open for 0% of the time, Pallas kernels for 0%

commit v1 on v0

--- a/solution.py
+++ b/solution.py
@@ -110,7 +110,9 @@
 
     def backward_partial(basis):
         operand = (row_scale[:, None] * basis).astype(jnp.bfloat16)
-        gathered = lax.all_gather(operand, FEAT, axis=0, tiled=True)
+        gathered = jnp.concatenate(
+            lax.all_to_all(jnp.stack([operand] * lax.axis_size(FEAT)), FEAT, 0, 0), axis=0
+        )
         return backward_local(tiles_here, scale_here, rows_here, cols_here, gathered, col_count)
 
     u_first, b_first = row_orthonormal(row_scale[:, None] * first_sums)

time: 890 us -> 872 us (0.980)
  waiting for transfers between devices: 385 us -> 350 us
  blocking collectives: 338 us -> 356 us
    all_gather x2 -> x0, waiting for transfers between devices: 39.8 us -> none  [backward_partial(): gathered = lax.all_gather(operand, FEAT, axis=0, tiled=True)]
    all_to_all x0 -> x1, blocking collectives: none -> 17.6 us  [backward_partial(): lax.all_to_all(jnp.stack([operand] * lax.axis_size(FEAT)), FEAT, 0, 0)]
    all_to_all x0 -> x1, waiting for transfers between devices: none -> 14.4 us  [backward_partial(): lax.all_to_all(jnp.stack([operand] * lax.axis_size(FEAT)), FEAT, 0, 0)]
  transfers between devices with their start and end apart: 9 -> 8, of which waited for: 9 -> 8; matrix products, arithmetic and copies ran while one was open for 0% -> 0% of each run, Pallas kernels for 0% -> 0%
where the time goes in v1:
time: 872 us; the launch traced here: 868 us
  blocking collectives  356 us (41%)
  waiting for transfers between devices  350 us (40%)
  other arithmetic  64.9 us (7%)
  matrix products  53 us (6%)
  local copies, waits for them, and re-layouts  25 us (3%)
  between operations  16.3 us (2%)
    psum x3, blocking collectives, all_sum(): return lax.psum(value, ('yh', 'x'))  119 us
    psum x3, blocking collectives, all_sum(): value = lax.psum(value, 'z')  91 us
    psum x1, waiting for transfers between devices, claim_sum(): part = lax.psum(part, ('yh', 'x'))  88 us
    reduce_scatter x1, waiting for transfers between devices, claim_scatter(): return lax.psum_scatter(part, ('yh', 'x'), scatter_dimension=0, tiled=True)  77.6 us
    all_gather x1, waiting for transfers between devices, claim_sum(): return lax.all_gather(part, 'z', axis=0, tiled=True)  40.9 us
    reduce_scatter x1, waiting for transfers between devices, claim_scatter(): part = lax.psum_scatter(blocks, 'z', scatter_dimension=0, tiled=True)  38.6 us
    reduce_scatter x1, waiting for transfers between devices, claim_sum(): part = lax.psum_scatter(value, 'z', scatter_dimension=0, tiled=True)  35 us
    unnamed x1, blocking collectives  32.8 us
  transfers between devices with their start and end apart: 8, of which 8 were waited for; matrix products, arithmetic and copies ran while one was open for 0% of the time, Pallas kernels for 0%

profile of v1, /device:TPU:16, one launch (start us, length us, event | category | flops | bytes accessed | tf_op | source)
XLA Modules:
  0.0 868.5 jit_solution(9460217736987644725)
XLA Ops:
  13.1 32.8 %all-reduce.1 = f32[4096]{0:T(1024)S(1)} all-reduce(f32[4096]{0:T(1024)S(1)} %convolution_bitcast_fusion.5), channel_id=3, replica_groups=mesh['yh'=2,'x'=4,'z'=8,'yl'=2,'c'=2] {'z'}, use_global_device_ids=true, to_apply=%region_3.0.clone | all-reduce | flops 4096 | bytes 32768
  47.2 21.5 %psum.91 = f32[512]{0:T(512)S(1)} all-reduce(f32[512]{0:T(512)S(1)} %dynamic-slice.3), channel_id=1, replica_groups=mesh['yh'=2,'x'=4,'z'=8,'yl'=2,'c'=2] {'yh','x'}, use_global_device_ids=true, to_apply=%region_4.0 | all-reduce | flops 512 | bytes 4096 | tf_op jit(solution)/shard_map/psum | solution.py:68
  68.6 20.8 %all-gather = f32[8,1,512]{2,1,0:T(1,128)S(1)} all-gather(f32[1,1,512]{2,1,0:T(1,128)S(1)} %bitcast.199), channel_id=1, replica_groups=mesh['yh'=2,'x'=4,'z'=8,'yl'=2,'c'=2] {'z'}, dimensions={0}, use_global_device_ids=true | all-gather | bytes 18432 | tf_op jit(solution)/shard_map/all_gather | solution.py:69
  89.7 10.9 %all-reduce.2 = (f32[64,64]{0,1:T(8,128)S(1)}, f32[8192]{0:T(1024)S(1)}) all-reduce(f32[64,64]{0,1:T(8,128)S(1)} %fusion.101, f32[8192]{0:T(1024)S(1)} %convolution_bitcast_fusion.4), channel_id=1, replica_groups=mesh['yh'=2,'x'=4,'z'=8,'yl'=2,'c'=2] {'yl','c'}, use_global_device_ids=true, to_apply=%region_5.0 | all-reduce | flops 12288 | bytes 98304 | tf_op jit(solution)/shard_map/psum | solution.py:101
  100.7 5.8 cholesky.89
  129.1 26.6 %reduce-scatter.6.cloned.1.call-done = f32[2048,64]{0,1:T(8,128)} async-done(((f32[8192,64]{0,1:T(8,128)}), f32[2048,64]{0,1:T(8,128)}) %reduce-scatter.6.cloned.1.call-update) | async-done | bytes 524304 | tf_op jit(solution)/shard_map/reduce_scatter | solution.py:105
  157.5 10.7 %psum.93 = f32[64,64]{0,1:T(8,128)S(1)} all-reduce(f32[64,64]{0,1:T(8,128)S(1)} %fusion.27), channel_id=1, replica_groups=mesh['yh'=2,'x'=4,'z'=8,'yl'=2,'c'=2] {'yl','c'}, use_global_device_ids=true, to_apply=%region_9.12 | all-reduce | flops 4096 | bytes 32768 | tf_op jit(solution)/shard_map/psum | solution.py:73
  168.2 30.2 %psum.94 = f32[64,64]{0,1:T(8,128)S(1)} all-reduce(f32[64,64]{0,1:T(8,128)S(1)} %psum.93), channel_id=1, replica_groups=mesh['yh'=2,'x'=4,'z'=8,'yl'=2,'c'=2] {'z'}, use_global_device_ids=true, to_apply=%region_10.13 | all-reduce | flops 4096 | bytes 32768 | tf_op jit(solution)/shard_map/psum | solution.py:74
  198.4 39.7 %psum.95 = f32[64,64]{0,1:T(8,128)S(1)} all-reduce(f32[64,64]{0,1:T(8,128)S(1)} %psum.94), channel_id=1, replica_groups=mesh['yh'=2,'x'=4,'z'=8,'yl'=2,'c'=2] {'yh','x'}, use_global_device_ids=true, to_apply=%region_11.14 | all-reduce | flops 4096 | bytes 32768 | tf_op jit(solution)/shard_map/psum | solution.py:75
  257.5 14.4 %all-to-all-done = bf16[4,2048,64]{1,2,0:T(8,128)(2,1)S(1)} async-done(((bf16[4,2048,64]{1,2,0:T(8,128)(2,1)}), bf16[4,2048,64]{1,2,0:T(8,128)(2,1)S(1)}, u32[]{:S(2)}, u32[]{:S(2)}) %all-to-all-start) | async-done | bytes 1048608 | tf_op jit(solution)/shard_map/all_to_all | solution.py:114
  284.0 35.0 %reduce-scatter.8.cloned.1.call-done = f32[512,64]{0,1:T(8,128)} async-done(((f32[4096,64]{0,1:T(8,128)}), f32[512,64]{0,1:T(8,128)}) %reduce-scatter.8.cloned.1.call-update) | async-done | bytes 131088 | tf_op jit(solution)/shard_map/reduce_scatter | solution.py:67
  319.1 88.0 %all-reduce.5.cloned.1.call-done = f32[512,64]{0,1:T(8,128)} async-done(((f32[512,64]{0,1:T(8,128)}), f32[512,64]{0,1:T(8,128)}) %all-reduce.5.cloned.1.call-update) | async-done | bytes 131088 | tf_op jit(solution)/shard_map/psum | solution.py:68
  407.2 40.9 %all-gather.3.cloned.1.call-done = f32[4096,64]{0,1:T(8,128)} async-done(((f32[512,64]{0,1:T(8,128)}), f32[4096,64]{0,1:T(8,128)}) %all-gather.3.cloned.1.call-update) | async-done | bytes 1048592 | tf_op jit(solution)/shard_map/all_gather | solution.py:69
  452.0 10.5 %psum.97 = f32[64,64]{0,1:T(8,128)S(1)} all-reduce(f32[64,64]{0,1:T(8,128)S(1)} %fusion.102), channel_id=1, replica_groups=mesh['yh'=2,'x'=4,'z'=8,'yl'=2,'c'=2] {'yl','c'}, use_global_device_ids=true, to_apply=%region_14.18 | all-reduce | flops 4096 | bytes 32768 | tf_op jit(solution)/shard_map/psum | solution.py:121
  489.7 28.9 %reduce-scatter.10.cloned.1.call-done = f32[2048,64]{0,1:T(8,128)} async-done(((f32[8192,64]{0,1:T(8,128)}), f32[2048,64]{0,1:T(8,128)}) %reduce-scatter.10.cloned.1.call-update) | async-done | bytes 524304 | tf_op jit(solution)/shard_map/reduce_scatter | solution.py:124
  521.5 10.7 %psum.98 = f32[64,64]{0,1:T(8,128)S(1)} all-reduce(f32[64,64]{0,1:T(8,128)S(1)} %fusion.103), channel_id=1, replica_groups=mesh['yh'=2,'x'=4,'z'=8,'yl'=2,'c'=2] {'yl','c'}, use_global_device_ids=true, to_apply=%region_16.20 | all-reduce | flops 4096 | bytes 32768 | tf_op jit(solution)/shard_map/psum | solution.py:73
  532.2 30.5 %psum.99 = f32[64,64]{0,1:T(8,128)S(1)} all-reduce(f32[64,64]{0,1:T(8,128)S(1)} %psum.98), channel_id=1, replica_groups=mesh['yh'=2,'x'=4,'z'=8,'yl'=2,'c'=2] {'z'}, use_global_device_ids=true, to_apply=%region_17.21 | all-reduce | flops 4096 | bytes 32768 | tf_op jit(solution)/shard_map/psum | solution.py:74
  562.8 39.2 %psum.100 = f32[64,64]{0,1:T(8,128)S(1)} all-reduce(f32[64,64]{0,1:T(8,128)S(1)} %psum.99), channel_id=1, replica_groups=mesh['yh'=2,'x'=4,'z'=8,'yl'=2,'c'=2] {'yh','x'}, use_global_device_ids=true, to_apply=%region_18.22 | all-reduce | flops 4096 | bytes 32768 | tf_op jit(solution)/shard_map/psum | solution.py:75
  615.7 17.6 %all_to_all.10 = bf16[4,2048,64]{1,2,0:T(8,128)(2,1)S(1)} all-to-all(bf16[4,2048,64]{1,2,0:T(8,128)(2,1)S(1)} %stack.30), channel_id=1, replica_groups=mesh['yh'=2,'x'=4,'z'=8,'yl'=2,'c'=2] {'yl','c'}, dimensions={0} | all-to-all | bytes 2097152 | tf_op jit(solution)/shard_map/all_to_all | solution.py:114
  648.8 38.6 %reduce-scatter.12.cloned.1.call-done = f32[512,64]{1,0:T(8,128)} async-done(((f32[4096,64]{1,0:T(8,128)}), f32[512,64]{1,0:T(8,128)}) %reduce-scatter.12.cloned.1.call-update) | async-done | bytes 131088 | tf_op jit(solution)/shard_map/reduce_scatter | solution.py:83
  687.5 77.6 %reduce-scatter.14.cloned.1.call-done = f32[64,64]{1,0:T(8,128)} async-done(((f32[512,64]{1,0:T(8,128)}), f32[64,64]{1,0:T(8,128)}) %reduce-scatter.14.cloned.1.call-update) | async-done | bytes 16400 | tf_op jit(solution)/shard_map/reduce_scatter | solution.py:84
  767.1 10.5 %psum.101 = f32[64,64]{0,1:T(8,128)S(1)} all-reduce(f32[64,64]{0,1:T(8,128)S(1)} %fusion.104), channel_id=1, replica_groups=mesh['yh'=2,'x'=4,'z'=8,'yl'=2,'c'=2] {'yl','c'}, use_global_device_ids=true, to_apply=%region_21.25 | all-reduce | flops 4096 | bytes 32768 | tf_op jit(solution)/shard_map/psum | solution.py:73
  777.7 30.2 %psum.102 = f32[64,64]{0,1:T(8,128)S(1)} all-reduce(f32[64,64]{0,1:T(8,128)S(1)} %psum.101), channel_id=1, replica_groups=mesh['yh'=2,'x'=4,'z'=8,'yl'=2,'c'=2] {'z'}, use_global_device_ids=true, to_apply=%region_22.26 | all-reduce | flops 4096 | bytes 32768 | tf_op jit(solution)/shard_map/psum | solution.py:74
  807.9 39.7 %psum.103 = f32[64,64]{0,1:T(8,128)S(1)} all-reduce(f32[64,64]{0,1:T(8,128)S(1)} %psum.102), channel_id=1, replica_groups=mesh['yh'=2,'x'=4,'z'=8,'yl'=2,'c'=2] {'yh','x'}, use_global_device_ids=true, to_apply=%region_23.27 | all-reduce | flops 4096 | bytes 32768 | tf_op jit(solution)/shard_map/psum | solution.py:75
  (126 shorter events, 140.9 us)
Async XLA Ops:
  7.2 1.3 copy-start
  7.2 38.7 %copy-start.10 = (u32[256]{0:T(256)S(1)}, u32[256]{0:T(256)}, u32[]{:S(2)}) copy-start(u32[256]{0:T(256)} %constant.80) | copy-start | bytes 3076
  7.2 5.7 copy-start.8
  7.2 5.7 copy-start.6
  7.2 82.3 %copy-start.7 = (s32[1,1,128]{2,1,0:T(1,128)S(1)}, s32[1,1,128]{2,1,0:T(1,128)}, u32[]{:S(2)}) copy-start(s32[1,1,128]{2,1,0:T(1,128)} %param.12) | copy-start | bytes 1540
  7.2 148.5 %reduce-scatter.6.cloned.1.call-start = ((), (), s32[]{:S(2)}) async-start(), calls=%async_computation.7 | async-start | bytes 2621440 | tf_op jit(solution)/shard_map/reduce_scatter | solution.py:105
  113.8 1.0 copy-start.2
  125.3 2.6 copy-start.9
  253.9 18.0 %all-to-all-start = ((bf16[4,2048,64]{1,2,0:T(8,128)(2,1)}), bf16[4,2048,64]{1,2,0:T(8,128)(2,1)S(1)}, u32[]{:S(2)}, u32[]{:S(2)}) async-start(bf16[4,2048,64]{1,2,0:T(8,128)(2,1)} %stack.14), calls=%async_computation.1 | async-start | bytes 2097152 | tf_op jit(solution)/shard_map/all_to_all | solution.py:114
  257.4 61.6 %reduce-scatter.8.cloned.1.call-start = ((), (), s32[]{:S(2)}) async-start(), calls=%async_computation.8 | async-start | bytes 1179648 | tf_op jit(solution)/shard_map/reduce_scatter | solution.py:67
  278.4 169.6 %copy-start.3 = (f32[4096,64]{0,1:T(8,128)S(1)}, f32[4096,64]{0,1:T(8,128)}, u32[]{:S(2)}) copy-start(f32[4096,64]{0,1:T(8,128)} %copy-done.2) | copy-start | bytes 3145732
  284.0 123.1 %all-reduce.5.cloned.1.call-start = ((), (), s32[]{:S(2)}) async-start(), calls=%async_computation.9 | async-start | bytes 262144 | tf_op jit(solution)/shard_map/psum | solution.py:68
  319.0 129.0 %all-gather.3.cloned.1.call-start = ((), (), s32[]{:S(2)}) async-start(), calls=%async_computation.10 | async-start | bytes 1179648 | tf_op jit(solution)/shard_map/all_gather | solution.py:69
  407.1 111.5 %reduce-scatter.10.cloned.1.call-start = ((), (), s32[]{:S(2)}) async-start(), calls=%async_computation.11 | async-start | bytes 2621440 | tf_op jit(solution)/shard_map/reduce_scatter | solution.py:124
  475.7 1.0 copy-start.4
  487.1 31.5 %copy-start.5 = (f32[2048,64]{0,1:T(8,128)S(1)}, f32[2048,64]{0,1:T(8,128)}, u32[]{:S(2)}) copy-start(f32[2048,64]{0,1:T(8,128)} %get-tuple-element.31) | copy-start | bytes 1572868
  489.7 197.7 %reduce-scatter.12.cloned.1.call-start = ((), (), s32[]{:S(2)}) async-start(), calls=%async_computation.12 | async-start | bytes 2359296 | tf_op jit(solution)/shard_map/reduce_scatter | solution.py:83
  644.8 216.6 %copy-start.1 = (f32[4096,64]{0,1:T(8,128)S(1)}, f32[4096,64]{0,1:T(8,128)}, u32[]{:S(2)}) copy-start(f32[4096,64]{0,1:T(8,128)} %param.14) | copy-start | bytes 3145732
  648.8 116.4 %reduce-scatter.14.cloned.1.call-start = ((), (), s32[]{:S(2)}) async-start(), calls=%async_computation.13 | async-start | bytes 294912 | tf_op jit(solution)/shard_map/reduce_scatter | solution.py:84
Sparse Core Ops, SparseCore 0:
  128.0 27.6 reduce-scatter.5
  284.1 34.8 reduce-scatter.7
  321.8 85.2 all-reduce.4
  408.7 39.2 all-gather.2
  489.8 28.7 reduce-scatter.9
  648.9 38.4 reduce-scatter.11
  691.8 73.3 reduce-scatter.13
